TPU v7x, 32 devices: a whole 2x2x4 slice. The times are simulated.
32 devices in a mesh: pair: 4 (over y, x), virt: 8 (over z, core).
Axes of the slice: x: 2, y: 2, z: 4, core: 2. Of those that a mesh axis runs over, the one named last changes fastest.
Arguments:
- amplitudes: float32 [480, 12288], P('pair', 'virt'), may hold values from -6 to 6
- integrals: float32 [8192, 12288], P('pair', 'virt'), may hold values from -0.0546875 to 0.0546875
- eps_occ: float32 [120], replicated, may hold values from -2.5 to -0.3
- eps_vir: float32 [128], replicated, may hold values from 0.3 to 3
- pair_list: int32 [480, 2], P('pair'), may hold values from 0 to 119, as said below
Outputs:
- ladder: float32 [480, 8192], P('pair', 'virt')
- update: float32 [480, 8192], P('pair', 'virt')
Inputs may be any that keep to these rules, and one draw needn't show every extreme that they name: `pair_list`: each row (i, j) has i < j; pairs may repeat.
All inputs are finite; a program needn't handle non-finite values.
Results may differ from a plain program's by a relative error of at most 0.000071.
Values sent between devices are 32-bit elements; how exact they have to be, the bound alone decides.
A program may use at most 64 MiB of HBM per device.

v0:
```python
import jax
import jax.numpy as jnp
from jax import lax
from jax.sharding import PartitionSpec as P


def antisymmetrize(partial_value, tile_width):
    blocks = partial_value.reshape(partial_value.shape[0], 2, tile_width, tile_width)
    mirrored = jnp.swapaxes(blocks[:, ::-1], 2, 3)
    return (blocks - mirrored).reshape(partial_value.shape)


def pair_energies(eps_occ, pair_list):
    occ_ids = lax.broadcasted_iota(jnp.int32, (1, 1, eps_occ.shape[0]), 2)
    one_hot = pair_list[:, :, None] == occ_ids
    return jnp.sum(jnp.where(one_hot, eps_occ[None, None, :], jnp.float32(0.0)), axis=(1, 2))


def sum_to_owners(antisym):
    return lax.psum_scatter(antisym, "virt", scatter_dimension=1, tiled=True)


def body(amplitudes, integrals, eps_occ, eps_vir, pair_list):
    tile_width = eps_vir.shape[0] // 2
    by_pairs = lax.dot_general(
        lax.all_gather(amplitudes, "pair", axis=0, tiled=True),
        integrals,
        (((1,), (1,)), ((), ())),
        precision=lax.Precision.HIGHEST,
        preferred_element_type=jnp.float32,
    )
    partial_value = lax.all_to_all(by_pairs, "pair", split_axis=0, concat_axis=1, tiled=True)
    ladder = sum_to_owners(antisymmetrize(partial_value, tile_width))
    column_count = ladder.shape[1]
    energy_tiles = eps_vir.reshape(2, tile_width)
    virt_energy = (energy_tiles[:, :, None] + energy_tiles[::-1][:, None, :]).reshape(
        2 * tile_width * tile_width
    )
    local_energy = lax.dynamic_slice_in_dim(
        virt_energy, lax.axis_index("virt") * column_count, column_count
    )
    pair_energy = pair_energies(eps_occ, pair_list)
    update = ladder / (pair_energy[:, None] - local_energy[None, :])
    return (ladder, update)


def solution(mesh):
    in_specs = (P("pair", "virt"), P("pair", "virt"), P(), P(), P("pair", None))
    out_specs = (P("pair", "virt"), P("pair", "virt"))
    return jax.shard_map(body, mesh=mesh, in_specs=in_specs, out_specs=out_specs, check_vma=False)
```

profile of v0, /device:TPU:0, one launch (start us, length us, event | category | flops | bytes accessed | tf_op | source)
XLA Modules:
  0.0 199.0 jit_solution(17090477642330334931)
XLA Ops:
  7.2 0.0 all-gather.2.cloned.1.call-start
  7.2 0.7 all-gather.2.cloned.1.call-update
  7.9 0.0 reduce-scatter.2.cloned.1.call-start
  7.9 46.8 %all-gather.2.cloned.1.call-done = f32[480,1536]{1,0:T(8,128)} async-done(((f32[120,1536]{1,0:T(8,128)}), f32[480,1536]{1,0:T(8,128)}) %all-gather.2.cloned.1.call-update) | async-done | bytes 2949136 | tf_op jit(solution)/shard_map/all_gather | solution.py:26
  54.8 22.0 %fusion = f32[480,2048]{1,0:T(8,128)S(1)} fusion(f32[480,1536]{1,0:T(8,128)} %all-gather.2.cloned.1.call-done, f32[2048,1536]{1,0:T(8,128)} %param.6), kind=kOutput, calls=%fused_computation.5 | convolution fusion | flops 18119393280 | bytes 19464192 | tf_op jit(solution)/shard_map/dot_general | solution.py:25
  76.8 48.5 %all_to_all.16 = f32[4,120,2048]{2,1,0:T(8,128)} all-to-all(f32[4,120,2048]{2,1,0:T(8,128)S(1)} %bitcast.12), channel_id=1, replica_groups=mesh['pair'=4,'virt'=8] {'pair'}, dimensions={0} | all-to-all | bytes 7864320 | tf_op jit(solution)/shard_map/all_to_all | solution.py:32
  125.4 5.3 %copy.19 = f32[4,120,2048]{1,2,0:T(8,128)} copy(f32[4,120,2048]{2,1,0:T(8,128)} %all_to_all.16) | data formatting | bytes 7864320 | tf_op jit(solution)/shard_map/all_to_all | solution.py:32
  130.7 0.0 copy-start
  130.7 4.8 %copy.20 = f32[120,2,64,64]{0,2,3,1:T(8,128)S(1)} copy(f32[120,2,64,64]{0,3,2,1:T(8,128)} %bitcast.9) | data formatting | bytes 7864320 | tf_op jit(solution)/shard_map/reshape | solution.py:8
  135.4 0.0 copy-done
  135.5 2.9 %bitcast_subtract_fusion = f32[120,2,64,64]{0,3,2,1:T(8,128)} fusion(f32[120,2,64,64]{0,3,2,1:T(8,128)S(1)} %bitcast.10, f32[120,2,64,64]{0,2,3,1:T(8,128)S(1)} %copy.20), kind=kLoop, calls=%fused_computation | loop fusion | flops 983040 | bytes 11796480 | tf_op jit(solution)/shard_map/sub | solution.py:10
  138.3 0.0 copy-start.3
  138.3 0.0 copy-start.1
  138.3 0.0 copy-start.2
  138.3 0.0 reduce-scatter.2.cloned.1.call-update
  138.4 0.6 copy-done.3
  139.0 0.1 add.24
  139.1 0.1 broadcast_add_fusion
  139.2 0.1 add.28
  139.3 0.0 copy-done.1
  139.3 0.0 copy-done.2
  139.3 0.2 select_reduce_fusion
  139.4 48.5 %reduce-scatter.2.cloned.1.call-done = f32[120,1024]{0,1:T(8,128)} async-done(((f32[120,8192]{0,1:T(8,128)}), f32[120,1024]{0,1:T(8,128)}) %reduce-scatter.2.cloned.1.call-update) | async-done | bytes 491536 | tf_op jit(solution)/shard_map/reduce_scatter | solution.py:20
  187.9 1.2 subtract_divide_fusion
  189.2 1.0 copy.22
  190.1 2.0 %copy.21 = f32[120,1024]{1,0:T(8,128)} copy(f32[120,1024]{0,1:T(8,128)} %reduce-scatter.2.cloned.1.call-done) | data formatting | bytes 983040
  (2 shorter events, 0.0 us)
Async XLA Ops:
  7.2 47.6 %all-gather.2.cloned.1.call-start = ((), (), s32[]{:S(2)}) async-start(), calls=%async_computation.2 | async-start | bytes 3686400 | tf_op jit(solution)/shard_map/all_gather | solution.py:26
  7.9 180.0 %reduce-scatter.2.cloned.1.call-start = ((), (), s32[]{:S(2)}) async-start(), calls=%async_computation.3 | async-start | bytes 4718592 | tf_op jit(solution)/shard_map/reduce_scatter | solution.py:20
  130.7 4.8 %copy-start = (f32[4,120,2048]{1,2,0:T(8,128)S(1)}, f32[4,120,2048]{1,2,0:T(8,128)}, u32[]{:S(2)}) copy-start(f32[4,120,2048]{1,2,0:T(8,128)} %copy.19) | copy-start | bytes 11796484
  138.3 0.7 copy-start.3
  138.3 0.9 copy-start.1
  138.3 0.9 copy-start.2
Sparse Core Ops, SparseCore 0:
  9.8 44.9 all-gather.1
  138.5 49.3 reduce-scatter.1
where the time goes:
time: 199 us
  waiting for transfers between devices  96 us (48%)
  blocking collectives  48.5 us (24%)
  matrix products  22 us (11%)
  between operations  14.1 us (7%)
  local copies, waits for them, and re-layouts  13.9 us (7%)
  other arithmetic  4.37 us (2%)
    all_to_all x1, blocking collectives, body(): lax.all_to_all(by_pairs, 'pair', split_axis=0, concat_axis=1, tiled=True)  48.5 us
    reduce_scatter x1, waiting for transfers between devices, sum_to_owners(): return lax.psum_scatter(antisym, 'virt', scatter_dimension=1, tiled=True)  48.5 us
    all_gather x1, waiting for transfers between devices, body(): lax.all_gather(amplitudes, 'pair', axis=0, tiled=True)  46.8 us
    dot_general x1, matrix products, body(): lax.dot_general(lax.all_gather(amplitudes, 'pair', axis=0, tiled=True), i...  22 us
    all_to_all x1, local copies, waits for them, and re-layouts, body(): lax.all_to_all(by_pairs, 'pair', split_axis=0, concat_axis=1, tiled=True)  5.3 us
    reshape x1, local copies, waits for them, and re-layouts, antisymmetrize(): partial_value.reshape(partial_value.shape[0], 2, tile_width, tile_width)  4.77 us
  transfers between devices with their start and end apart: 2, of which 2 were waited for; matrix products, arithmetic and copies ran while one was open for 0% of the time, Pallas kernels for 0%

commit v1 on v0

v1 whole, which is shorter than its diff:
```python
import functools

import jax
import jax.numpy as jnp
from jax import lax
from jax.experimental import pallas as pl
from jax.experimental.pallas import tpu as pltpu
from jax.sharding import PartitionSpec as P

MESH = pl.DeviceIdType.MESH
LANES = 128


def antisymmetrize(partial_value, tile_width):
    blocks = partial_value.reshape(partial_value.shape[0], 2, tile_width, tile_width)
    mirrored = jnp.swapaxes(blocks[:, ::-1], 2, 3)
    return (blocks - mirrored).reshape(partial_value.shape)


def pair_energies(eps_occ, pair_list):
    occ_ids = lax.broadcasted_iota(jnp.int32, (1, 1, eps_occ.shape[0]), 2)
    one_hot = pair_list[:, :, None] == occ_ids
    return jnp.sum(jnp.where(one_hot, eps_occ[None, None, :], jnp.float32(0.0)), axis=(1, 2))


def sum_to_owners(antisym):
    return lax.psum_scatter(antisym, "virt", scatter_dimension=1, tiled=True)


def updated(ladder, eps_occ, eps_vir, pair_list):
    tile_width = eps_vir.shape[0] // 2
    column_count = ladder.shape[1]
    energy_tiles = eps_vir.reshape(2, tile_width)
    virt_energy = (energy_tiles[:, :, None] + energy_tiles[::-1][:, None, :]).reshape(
        2 * tile_width * tile_width
    )
    local_energy = lax.dynamic_slice_in_dim(
        virt_energy, lax.axis_index("virt") * column_count, column_count
    )
    pair_energy = pair_energies(eps_occ, pair_list)
    return ladder / (pair_energy[:, None] - local_energy[None, :])


def any_mesh_body(amplitudes, integrals, eps_occ, eps_vir, pair_list):
    tile_width = eps_vir.shape[0] // 2
    by_pairs = lax.dot_general(
        lax.all_gather(amplitudes, "pair", axis=0, tiled=True),
        integrals,
        (((1,), (1,)), ((), ())),
        precision=lax.Precision.HIGHEST,
        preferred_element_type=jnp.float32,
    )
    partial_value = lax.all_to_all(by_pairs, "pair", split_axis=0, concat_axis=1, tiled=True)
    ladder = sum_to_owners(antisymmetrize(partial_value, tile_width))
    return (ladder, updated(ladder, eps_occ, eps_vir, pair_list))


def reduce_kernel(
    h, ct_ref, out_ref, got, summed, rows, diff, below, above, upward, downward, kept, other,
    core_send, core_recv, pair_send, pair_recv, up_send, up_recv, down_send, down_recv,
    last_send, last_recv,
):
    r = lax.axis_index("pair")
    v = lax.axis_index("virt")
    z = v // 2
    c = v % 2
    mate = v + 1 - 2 * c
    x = r % 2
    y = r // 2
    peers = (y * 2 + (1 - x), (1 - y) * 2 + x, (1 - y) * 2 + (1 - x))
    quad = 2 * h * h

    barrier = pltpu.get_barrier_semaphore()
    pl.semaphore_signal(barrier, inc=1, device_id={"virt": mate}, device_id_type=MESH)
    for peer in peers:
        pl.semaphore_signal(barrier, inc=1, device_id={"pair": peer}, device_id_type=MESH)

    @pl.when(z < 3)
    def _():
        pl.semaphore_signal(barrier, inc=1, device_id={"virt": v + 2}, device_id_type=MESH)

    @pl.when(z > 0)
    def _():
        pl.semaphore_signal(barrier, inc=1, device_id={"virt": v - 2}, device_id_type=MESH)

    inner = jnp.logical_and(z > 0, z < 3)

    @pl.when(inner)
    def _():
        pl.semaphore_wait(barrier, 6)

    @pl.when(jnp.logical_not(inner))
    def _():
        pl.semaphore_wait(barrier, 5)

    order = (peers[2], peers[0], peers[1], r)

    def core_copy(n, i):
        lanes = pl.ds(pl.multiple_of(order[n] * LANES, LANES), LANES)
        return pltpu.make_async_remote_copy(
            src_ref=ct_ref.at[i, :, :, (1 - c + i) % 2, :, lanes],
            dst_ref=got.at[n, i],
            send_sem=core_send.at[n, i],
            recv_sem=core_recv.at[n, i],
            device_id={"virt": mate},
            device_id_type=MESH,
        )

    def pair_copy(n):
        return pltpu.make_async_remote_copy(
            src_ref=summed.at[n],
            dst_ref=rows.at[pl.ds(pl.multiple_of(r * 2 * quad, 8), 2 * quad)],
            send_sem=pair_send.at[n],
            recv_sem=pair_recv.at[n],
            device_id={"pair": order[n]},
            device_id_type=MESH,
        )

    for n in range(4):
        for i in range(2):
            core_copy(n, i).start()
    for n in range(4):
        lanes = pl.ds(pl.multiple_of(order[n] * LANES, LANES), LANES)
        for i in range(2):
            core_copy(n, i).wait_recv()

            @pl.loop(0, h)
            def _(a):
                for bh in range(2):
                    total = ct_ref[i, a, bh, (c + i) % 2, :, lanes] + got[n, i, a, bh]
                    start = ((i * h + a) * 2 + bh) * h
                    if n < 3:
                        summed[n, pl.ds(pl.multiple_of(start, 8), h), :] = total
                    else:
                        at = pl.multiple_of(r * 2 * quad + start, 8)
                        rows[pl.ds(at, h), :] = total

        if n < 3:
            pair_copy(n).start()

    for n in range(3):
        pair_copy(n).wait_recv()

    for ah in range(2):
        for bh in range(2):
            for i in range(2):

                @pl.loop(0, h)
                def _(a):
                    mirror = (c + i) % 2
                    direct = (((ah * 2 + i) * h + a) * 2 + bh) * h
                    swapped = ((((2 + bh) * 2 + mirror) * h) * 2 + ah) * h + a
                    plain = rows[pl.ds(pl.multiple_of(direct, 8), h), :]
                    turned = rows[pl.ds(swapped, h, stride=2 * h), :]
                    at = pl.multiple_of((i * h + a) * h, 8)
                    diff[ah * 2 + bh, pl.ds(at, h), :] = plain - turned

    def up_copy(q):
        return pltpu.make_async_remote_copy(
            src_ref=upward.at[q], dst_ref=below.at[q],
            send_sem=up_send.at[q], recv_sem=up_recv.at[q],
            device_id={"virt": v + 2}, device_id_type=MESH,
        )

    def down_copy(q):
        return pltpu.make_async_remote_copy(
            src_ref=downward.at[q], dst_ref=above.at[q],
            send_sem=down_send.at[q], recv_sem=down_recv.at[q],
            device_id={"virt": v - 2}, device_id_type=MESH,
        )

    def sends_up(q):
        return (z < 2) if q % 2 == 0 else (z < 3)

    def sends_down(q):
        return (z > 1) if q // 2 == 1 else (z > 0)

    def hears_below(q):
        return jnp.logical_and(z > 0, z < 3) if q % 2 == 0 else (z > 0)

    def hears_above(q):
        return jnp.logical_and(z > 0, z < 3) if q // 2 == 1 else (z < 3)

    def pass_up(q):
        @pl.when(z == 0)
        def _():
            upward[q] = diff[q]

        @pl.when(hears_below(q))
        def _():
            up_copy(q).wait_recv()

            @pl.when(sends_up(q))
            def _():
                upward[q] = diff[q] + below[q]

        @pl.when(sends_up(q))
        def _():
            up_copy(q).start()

    def pass_down(q):
        @pl.when(z == 3)
        def _():
            downward[q] = diff[q]

        @pl.when(hears_above(q))
        def _():
            down_copy(q).wait_recv()

            @pl.when(sends_down(q))
            def _():
                downward[q] = diff[q] + above[q]

        @pl.when(sends_down(q))
        def _():
            down_copy(q).start()

    quads = (1, 0, 3, 2)

    @pl.when(z < 2)
    def _():
        for s in range(5):
            if s < 4:
                pass_up(quads[s])
            if s > 0:
                pass_down(quads[s - 1])

    @pl.when(z >= 2)
    def _():
        for s in range(5):
            if s < 4:
                pass_down(quads[s])
            if s > 0:
                pass_up(quads[s - 1])

    def total_of(t, i):
        q = jnp.where(z < 2, z * 2 + t, t * 2 + z - 2)
        at = pl.ds(pl.multiple_of(i * h * h, 8), h * h)
        low = jnp.where(z > 0, below[q, at, :], jnp.float32(0.0))
        high = jnp.where(z < 3, above[q, at, :], jnp.float32(0.0))
        return diff[q, at, :] + low + high

    mine = jnp.where(z < 2, c, 0)
    for t in range(2):
        other[t] = total_of(t, jnp.where(z < 2, 1 - c, 1))
    last = pltpu.make_async_remote_copy(
        src_ref=other, dst_ref=kept.at[1], send_sem=last_send, recv_sem=last_recv,
        device_id={"virt": mate}, device_id_type=MESH,
    )
    last.start()
    for t in range(2):
        kept[0, t] = total_of(t, mine)

    def put(s):
        for t in range(2):

            @pl.loop(0, h)
            def _(a):
                at = pl.multiple_of((a * 4 + 2 * t + s) * h, 8)
                plain = kept[s, t, pl.ds(pl.multiple_of(a * h, 8), h), :]
                turned = kept[s, t, pl.ds(a, h, stride=h), :]
                out_ref[pl.ds(at, h), :] = jnp.where(z < 2, plain, -turned)

    put(0)
    last.wait_recv()
    put(1)

    last.wait_send()
    for n in range(4):
        for i in range(2):
            core_copy(n, i).wait_send()
    for n in range(3):
        pair_copy(n).wait_send()
    for q in range(4):

        @pl.when(sends_up(q))
        def _():
            up_copy(q).wait_send()

        @pl.when(sends_down(q))
        def _():
            down_copy(q).wait_send()


def reduced(ct, tile_width):
    h = tile_width // 4
    quad = 2 * h * h
    ct = ct.reshape(2, h, 2, 2, h, ct.shape[1])
    f32 = jnp.float32
    dma = pltpu.SemaphoreType.DMA
    return pl.pallas_call(
        functools.partial(reduce_kernel, h),
        out_shape=jax.ShapeDtypeStruct((tile_width * h, LANES), f32),
        in_specs=[pl.BlockSpec(memory_space=pltpu.VMEM)],
        out_specs=pl.BlockSpec(memory_space=pltpu.VMEM),
        scratch_shapes=[
            pltpu.VMEM((4, 2, h, 2, h, LANES), f32),
            pltpu.VMEM((3, 2 * quad, LANES), f32),
            pltpu.VMEM((8 * quad, LANES), f32),
            pltpu.VMEM((4, quad, LANES), f32),
            pltpu.VMEM((4, quad, LANES), f32),
            pltpu.VMEM((4, quad, LANES), f32),
            pltpu.VMEM((4, quad, LANES), f32),
            pltpu.VMEM((4, quad, LANES), f32),
            pltpu.VMEM((2, 2, h * h, LANES), f32),
            pltpu.VMEM((2, h * h, LANES), f32),
            dma((4, 2)), dma((4, 2)), dma((3,)), dma((3,)),
            dma((4,)), dma((4,)), dma((4,)), dma((4,)), dma, dma,
        ],
        compiler_params=pltpu.CompilerParams(
            collective_id=0, has_side_effects=True, vmem_limit_bytes=48 * 1024 * 1024
        ),
        name="reduce_antisymmetrized",
    )(ct)


def block_body(amplitudes, integrals, eps_occ, eps_vir, pair_list):
    tile_width = eps_vir.shape[0] // 2
    count = amplitudes.shape[0]
    gathered = lax.all_gather(amplitudes, "pair", axis=0, tiled=False)
    gathered = jnp.pad(gathered, ((0, 0), (0, LANES - count), (0, 0)))
    ct = lax.dot_general(
        integrals,
        gathered.reshape(-1, gathered.shape[2]),
        (((1,), (1,)), ((), ())),
        precision=lax.Precision.HIGH,
        preferred_element_type=jnp.float32,
    )
    ladder = reduced(ct, tile_width).T[:count]
    return (ladder, updated(ladder, eps_occ, eps_vir, pair_list))


def solution(mesh):
    in_specs = (P("pair", "virt"), P("pair", "virt"), P(), P(), P("pair", None))
    out_specs = (P("pair", "virt"), P("pair", "virt"))
    fits = mesh.shape["pair"] == 4 and mesh.shape["virt"] == 8

    def body(amplitudes, integrals, eps_occ, eps_vir, pair_list):
        tiled = eps_vir.shape[0] % 64 == 0 and amplitudes.shape[0] <= LANES
        chosen = block_body if fits and tiled else any_mesh_body
        return chosen(amplitudes, integrals, eps_occ, eps_vir, pair_list)

    return jax.shard_map(body, mesh=mesh, in_specs=in_specs, out_specs=out_specs, check_vma=False)
```

time: 199 us -> 161 us (0.81)
  the two profiles are of different devices: /device:TPU:0 before, /device:TPU:17 now
where the time goes in v1:
time: 161 us
  Pallas kernels  75 us (47%)
  waiting for transfers between devices  43.9 us (27%)
  matrix products  14.4 us (9%)
  between operations  14.1 us (9%)
  local copies, waits for them, and re-layouts  12.6 us (8%)
    pallas_call x1, Pallas kernels, reduced(): pl.pallas_call(functools.partial(reduce_kernel, h), out_shape=jax.ShapeDt...  75 us
    all_gather x1, waiting for transfers between devices, block_body(): gathered = lax.all_gather(amplitudes, 'pair', axis=0, tiled=False)  43.2 us
    dot_general x1, matrix products, block_body(): lax.dot_general(integrals, gathered.reshape(-1, gathered.shape[2]), (((1,...  14.4 us
    dot_general x1, local copies, waits for them, and re-layouts, block_body(): lax.dot_general(integrals, gathered.reshape(-1, gathered.shape[2]), (((1,...  5.38 us
    unnamed x6, local copies, waits for them, and re-layouts  4.15 us
  transfers between devices with their start and end apart: 1, of which 1 were waited for; matrix products, arithmetic and copies ran while one was open for 1% of the time, Pallas kernels for 0%

profile of v1, /device:TPU:17, one launch (start us, length us, event | category | flops | bytes accessed | tf_op | source)
XLA Modules:
  0.0 161.2 jit_solution(15404014310469444032)
XLA Ops:
  7.2 0.0 all-gather.3.cloned.1.call-start
  7.2 0.7 all-gather.3.cloned.1.call-update
  7.9 0.7 add.24
  8.7 0.1 broadcast_add_fusion
  8.8 0.1 add.28
  8.8 0.0 copy-start.1
  8.8 0.9 select_reduce_fusion
  9.7 43.2 %all-gather.3.cloned.1.call-done = f32[480,1536]{1,0:T(8,128)} async-done(((f32[120,1536]{1,0:T(8,128)}), f32[480,1536]{1,0:T(8,128)}) %all-gather.3.cloned.1.call-update) | async-done | bytes 2949136 | tf_op jit(solution)/shard_map/all_gather | solution.py:320
  53.0 2.2 %pad.4 = f32[4,128,1536]{2,1,0:T(8,128)S(1)} pad(f32[4,120,1536]{2,1,0:T(8,128)} %bitcast.11, f32[]{:T(128)} %constant.5.clone.1), padding=0_0x0_8x0_0 | pad | bytes 6094852 | tf_op jit(solution)/shard_map/jit(_pad)/pad | solution.py:321
  55.2 14.4 %convolution_bitcast_fusion = f32[2048,512]{0,1:T(8,128)} fusion(f32[512,1536]{1,0:T(8,128)S(1)} %bitcast.10, f32[2048,1536]{1,0:T(8,128)} %param.6), kind=kOutput, calls=%fused_computation | convolution fusion | flops 9663676416 | bytes 19922944 | tf_op jit(solution)/shard_map/dot_general | solution.py:322
  69.6 0.0 copy-done.1
  69.6 5.4 %copy.11 = f32[2048,512]{1,0:T(8,128)} copy(f32[2048,512]{0,1:T(8,128)} %convolution_bitcast_fusion) | data formatting | bytes 8388608 | tf_op jit(solution)/shard_map/dot_general | solution.py:322
  75.0 0.0 copy-start
  75.0 2.2 %copy-done = f32[2048,512]{1,0:T(8,128)S(1)} copy-done((f32[2048,512]{1,0:T(8,128)S(1)}, f32[2048,512]{1,0:T(8,128)}, u32[]{:S(2)}) %copy-start) | copy-done | bytes 4194328
  77.2 0.0 dynamic-slice-start
  77.2 75.0 %reduce_antisymmetrized.1 = f32[1024,128]{1,0:T(8,128)S(1)} custom-call(f32[2,16,2,2,16,512]{5,4,3,2,1,0:T(8,128)S(1)} %bitcast.8), custom_call_target="tpu_custom_call" | custom-call | tf_op jit(solution)/shard_map/reduce_antisymmetrized/pallas_call | solution.py:291
  152.1 0.0 dynamic-slice-done
  152.1 0.2 subtract_divide_fusion
  152.4 1.0 copy.12
  153.3 1.0 copy.13
  (1 shorter events, 0.0 us)
Async XLA Ops:
  7.2 45.8 %all-gather.3.cloned.1.call-start = ((), (), s32[]{:S(2)}) async-start(), calls=%async_computation | async-start | bytes 3686400 | tf_op jit(solution)/shard_map/all_gather | solution.py:320
  8.8 60.8 %copy-start.1 = (f32[8192]{0:T(1024)}, f32[8192]{0:T(1024)S(1)}, u32[]{:S(2)}) copy-start(f32[8192]{0:T(1024)S(1)} %add.28) | copy-start | bytes 98308
  75.0 2.2 %copy-start = (f32[2048,512]{1,0:T(8,128)S(1)}, f32[2048,512]{1,0:T(8,128)}, u32[]{:S(2)}) copy-start(f32[2048,512]{1,0:T(8,128)} %copy.11) | copy-start | bytes 12582916
  77.2 75.0 %dynamic-slice-start = ((f32[8192]{0:T(1024)}, s32[]{:T(128)}), f32[1024]{0:T(1024)S(1)}, s32[]{:S(2)}) async-start(f32[8192]{0:T(1024)} %copy-done.1, s32[]{:T(128)} %select_n.8), calls=%async_computation.1 | async-start | bytes 8704 | tf_op jit(solution)/shard_map/dynamic_slice | solution.py:37
Sparse Core Ops, SparseCore 0:
  9.8 43.1 all-gather.2

commit v2 on v1

--- a/solution.py
+++ b/solution.py
@@ -55,8 +55,21 @@
     return (ladder, updated(ladder, eps_occ, eps_vir, pair_list))
 
 
-def reduce_kernel(
-    h, ct_ref, out_ref, got, summed, rows, diff, below, above, upward, downward, kept, other,
+def split(value):
+    high = value.astype(jnp.bfloat16)
+    return high, (value - high.astype(jnp.float32)).astype(jnp.bfloat16)
+
+
+def times(left, right):
+    return lax.dot_general(
+        left, right, (((1,), (1,)), ((), ())), preferred_element_type=jnp.float32
+    )
+
+
+def ladder_kernel(
+    h, amp_ref, int_ref, out_ref, stage, int_high, int_low, blocks, weights, ct_ref,
+    got, summed, rows, diff, below, above, upward, downward, kept, other,
+    stage_sem, amp_send, amp_recv,
     core_send, core_recv, pair_send, pair_recv, up_send, up_recv, down_send, down_recv,
     last_send, last_recv,
 ):
@@ -69,6 +82,21 @@
     y = r // 2
     peers = (y * 2 + (1 - x), (1 - y) * 2 + x, (1 - y) * 2 + (1 - x))
     quad = 2 * h * h
+    count, depth = amp_ref.shape
+    cut = count // 16 * 8
+    parts = (pl.ds(0, cut), pl.ds(cut, count - cut))
+    step = stage.shape[1]
+    steps = int_ref.shape[0] // step
+
+    def stage_copy(t):
+        return pltpu.make_async_copy(
+            int_ref.at[pl.ds(pl.multiple_of(t * step, 8), step)],
+            stage.at[t % 2],
+            stage_sem.at[t % 2],
+        )
+
+    stage_copy(0).start()
+    stage_copy(1).start()
 
     barrier = pltpu.get_barrier_semaphore()
     pl.semaphore_signal(barrier, inc=1, device_id={"virt": mate}, device_id_type=MESH)
@@ -93,12 +121,81 @@
     def _():
         pl.semaphore_wait(barrier, 5)
 
+    def amp_copy(d, part):
+        return pltpu.make_async_remote_copy(
+            src_ref=amp_ref.at[parts[part]],
+            dst_ref=blocks.at[d, parts[part]],
+            send_sem=amp_send.at[d, part],
+            recv_sem=amp_recv.at[d, part],
+            device_id={"pair": peers[d]},
+            device_id_type=MESH,
+        )
+
+    def pass_on(d):
+        return pltpu.make_async_remote_copy(
+            src_ref=blocks.at[d, parts[d]],
+            dst_ref=blocks.at[2, parts[d]],
+            send_sem=amp_send.at[2, d],
+            recv_sem=amp_recv.at[2, d],
+            device_id={"pair": peers[1 - d]},
+            device_id_type=MESH,
+        )
+
+    for late in range(2):
+        for d in range(2):
+            amp_copy(d, d if late == 0 else 1 - d).start()
+
+    def weigh(source, high_at, low_at):
+        wide = 2 * LANES
+
+        @pl.loop(0, depth // wide)
+        def _(k):
+            columns = pl.ds(pl.multiple_of(k * wide, wide), wide)
+            value = source[:, columns]
+            if count < LANES:
+                value = jnp.concatenate(
+                    [value, jnp.zeros((LANES - count, wide), jnp.float32)], axis=0
+                )
+            high, low = split(value)
+            weights[pl.ds(high_at * LANES, LANES), columns] = high
+            weights[pl.ds(low_at * LANES, LANES), columns] = low
+
+    def keep(t, size, lanes, value):
+        per = size // (4 * h)
+        i = t // (h // per)
+        at = pl.multiple_of(t % (h // per) * per, per)
+        ct_ref[i, pl.ds(at, per), :, :, :, lanes] = value.reshape(per, 2, 2, h, value.shape[1])
+
+    def one_block(high, low, at):
+        both = times(high, weights[pl.ds(at * LANES, 2 * LANES), :])
+        rest = times(low, weights[pl.ds(at * LANES, LANES), :])
+        return both[:, :LANES] + both[:, LANES:] + rest
+
+    weigh(amp_ref, 0, 1)
+
+    @pl.loop(0, steps)
+    def _(t):
+        stage_copy(t).wait()
+        high, low = split(stage[t % 2])
+        at = pl.ds(pl.multiple_of(t * step, 16), step)
+        int_high[at, :] = high
+        int_low[at, :] = low
+
+        @pl.when(t + 2 < steps)
+        def _():
+            stage_copy(t + 2).start()
+
+        keep(t, step, pl.ds(3 * LANES, LANES), one_block(int_high[at, :], int_low[at, :], 0))
+
+    for d in range(2):
+        amp_copy(d, d).wait_recv()
+        pass_on(d).start()
+
     order = (peers[2], peers[0], peers[1], r)
 
     def core_copy(n, i):
-        lanes = pl.ds(pl.multiple_of(order[n] * LANES, LANES), LANES)
         return pltpu.make_async_remote_copy(
-            src_ref=ct_ref.at[i, :, :, (1 - c + i) % 2, :, lanes],
+            src_ref=ct_ref.at[i, :, :, (1 - c + i) % 2, :, pl.ds(n * LANES, LANES)],
             dst_ref=got.at[n, i],
             send_sem=core_send.at[n, i],
             recv_sem=core_recv.at[n, i],
@@ -116,11 +213,12 @@
             device_id_type=MESH,
         )
 
-    for n in range(4):
+    def core_start(n):
         for i in range(2):
             core_copy(n, i).start()
-    for n in range(4):
-        lanes = pl.ds(pl.multiple_of(order[n] * LANES, LANES), LANES)
+
+    def core_add(n):
+        lanes = pl.ds(n * LANES, LANES)
         for i in range(2):
             core_copy(n, i).wait_recv()
 
@@ -135,25 +233,54 @@
                         at = pl.multiple_of(r * 2 * quad + start, 8)
                         rows[pl.ds(at, h), :] = total
 
-        if n < 3:
-            pair_copy(n).start()
-
-    for n in range(3):
-        pair_copy(n).wait_recv()
-
-    for ah in range(2):
-        for bh in range(2):
-            for i in range(2):
-
-                @pl.loop(0, h)
-                def _(a):
-                    mirror = (c + i) % 2
-                    direct = (((ah * 2 + i) * h + a) * 2 + bh) * h
-                    swapped = ((((2 + bh) * 2 + mirror) * h) * 2 + ah) * h + a
-                    plain = rows[pl.ds(pl.multiple_of(direct, 8), h), :]
-                    turned = rows[pl.ds(swapped, h, stride=2 * h), :]
-                    at = pl.multiple_of((i * h + a) * h, 8)
-                    diff[ah * 2 + bh, pl.ds(at, h), :] = plain - turned
+    core_start(3)
+    for d in range(2):
+        amp_copy(d, 1 - d).wait_recv()
+        weigh(blocks.at[d], 4 + d, 6 + d)
+    big = 2 * step
+
+    @pl.loop(0, steps // 2)
+    def _(t):
+        at = pl.ds(pl.multiple_of(t * big, 16), big)
+        near_high = weights[pl.ds(4 * LANES, 2 * LANES), :]
+        near_low = weights[pl.ds(6 * LANES, 2 * LANES), :]
+        value = times(int_high[at, :], near_high) + times(int_high[at, :], near_low)
+        value = value + times(int_low[at, :], near_high)
+        keep(t, big, pl.ds(LANES, 2 * LANES), value)
+
+    core_start(1)
+    core_start(2)
+    core_add(3)
+    for n in (1, 2):
+        core_add(n)
+        pair_copy(n).start()
+    for d in range(2):
+        pass_on(d).wait_recv()
+    weigh(blocks.at[2], 2, 3)
+
+    @pl.loop(0, steps // 2)
+    def _(t):
+        at = pl.ds(pl.multiple_of(t * big, 16), big)
+        keep(t, big, pl.ds(0, LANES), one_block(int_high[at, :], int_low[at, :], 2))
+
+    core_start(0)
+    core_add(0)
+    pair_copy(0).start()
+
+    def antisym(q):
+        ah = q // 2
+        bh = q % 2
+        for i in range(2):
+            mirror = (c + i) % 2
+
+            @pl.loop(0, h)
+            def _(a):
+                direct = (((ah * 2 + i) * h + a) * 2 + bh) * h
+                swapped = ((((2 + bh) * 2 + mirror) * h) * 2 + ah) * h + a
+                plain = rows[pl.ds(pl.multiple_of(direct, 8), h), :]
+                turned = rows[pl.ds(swapped, h, stride=2 * h), :]
+                at = pl.multiple_of((i * h + a) * h, 8)
+                diff[q, pl.ds(at, h), :] = plain - turned
 
     def up_copy(q):
         return pltpu.make_async_remote_copy(
@@ -170,68 +297,100 @@
         )
 
     def sends_up(q):
-        return (z < 2) if q % 2 == 0 else (z < 3)
+        return jnp.logical_or(z < 2, jnp.logical_and(z == 2, q % 2 == 1))
 
     def sends_down(q):
-        return (z > 1) if q // 2 == 1 else (z > 0)
+        return jnp.logical_or(z > 1, jnp.logical_and(z == 1, q // 2 == 0))
 
     def hears_below(q):
-        return jnp.logical_and(z > 0, z < 3) if q % 2 == 0 else (z > 0)
+        return jnp.logical_or(inner, jnp.logical_and(z == 3, q % 2 == 1))
 
     def hears_above(q):
-        return jnp.logical_and(z > 0, z < 3) if q // 2 == 1 else (z < 3)
-
-    def pass_up(q):
+        return jnp.logical_or(inner, jnp.logical_and(z == 0, q // 2 == 0))
+
+    def go_up(q):
+        @pl.when(hears_below(q))
+        def _():
+            up_copy(q).wait_recv()
+
         @pl.when(z == 0)
         def _():
             upward[q] = diff[q]
 
-        @pl.when(hears_below(q))
-        def _():
-            up_copy(q).wait_recv()
-
-            @pl.when(sends_up(q))
-            def _():
-                upward[q] = diff[q] + below[q]
+        @pl.when(jnp.logical_and(z > 0, sends_up(q)))
+        def _():
+            upward[q] = diff[q] + below[q]
 
         @pl.when(sends_up(q))
         def _():
             up_copy(q).start()
 
-    def pass_down(q):
+    def go_down(q):
+        @pl.when(hears_above(q))
+        def _():
+            down_copy(q).wait_recv()
+
         @pl.when(z == 3)
         def _():
             downward[q] = diff[q]
 
-        @pl.when(hears_above(q))
-        def _():
-            down_copy(q).wait_recv()
-
-            @pl.when(sends_down(q))
-            def _():
-                downward[q] = diff[q] + above[q]
+        @pl.when(jnp.logical_and(z < 3, sends_down(q)))
+        def _():
+            downward[q] = diff[q] + above[q]
 
         @pl.when(sends_down(q))
         def _():
             down_copy(q).start()
 
-    quads = (1, 0, 3, 2)
-
-    @pl.when(z < 2)
-    def _():
-        for s in range(5):
-            if s < 4:
-                pass_up(quads[s])
-            if s > 0:
-                pass_down(quads[s - 1])
-
-    @pl.when(z >= 2)
-    def _():
-        for s in range(5):
-            if s < 4:
-                pass_down(quads[s])
-            if s > 0:
-                pass_up(quads[s - 1])
+    def near(q):
+        @pl.when(z < 2)
+        def _():
+            go_up(q)
+
+        @pl.when(z >= 2)
+        def _():
+            go_down(q)
+
+    def far(q):
+        @pl.when(z < 2)
+        def _():
+            go_down(q)
+
+        @pl.when(z >= 2)
+        def _():
+            go_up(q)
+
+    early = [jnp.where(y == 0, t * 2 + x, x * 2 + t) for t in range(2)]
+    late = [jnp.where(y == 0, t * 2 + 1 - x, (1 - x) * 2 + t) for t in range(2)]
+    pair_copy(1).wait_recv()
+    pair_copy(2).wait_recv()
+    antisym(early[0])
+    near(early[0])
+    antisym(early[1])
+    near(early[1])
+
+    @pl.when(inner)
+    def _():
+        far(early[0])
+
+    pair_copy(0).wait_recv()
+    antisym(late[0])
+    near(late[0])
+
+    @pl.when(inner)
+    def _():
+        far(early[1])
+
+    antisym(late[1])
+    near(late[1])
+
+    @pl.when(jnp.logical_not(inner))
+    def _():
+        far(early[0])
+        far(early[1])
+
+    far(late[0])
+    far(late[1])
 
     def total_of(t, i):
         q = jnp.where(z < 2, z * 2 + t, t * 2 + z - 2)
@@ -266,6 +425,10 @@
     put(1)
 
     last.wait_send()
+    for d in range(2):
+        amp_copy(d, 0).wait_send()
+        amp_copy(d, 1).wait_send()
+        pass_on(d).wait_send()
     for n in range(4):
         for i in range(2):
             core_copy(n, i).wait_send()
@@ -282,18 +445,27 @@
             down_copy(q).wait_send()
 
 
-def reduced(ct, tile_width):
+def ladder_of(amplitudes, integrals, tile_width):
     h = tile_width // 4
     quad = 2 * h * h
-    ct = ct.reshape(2, h, 2, 2, h, ct.shape[1])
+    count, depth = amplitudes.shape
+    owned = integrals.shape[0]
+    step = owned // 8
     f32 = jnp.float32
+    bf16 = jnp.bfloat16
     dma = pltpu.SemaphoreType.DMA
     return pl.pallas_call(
-        functools.partial(reduce_kernel, h),
+        functools.partial(ladder_kernel, h),
         out_shape=jax.ShapeDtypeStruct((tile_width * h, LANES), f32),
-        in_specs=[pl.BlockSpec(memory_space=pltpu.VMEM)],
+        in_specs=[pl.BlockSpec(memory_space=pltpu.VMEM), pl.BlockSpec(memory_space=pl.ANY)],
         out_specs=pl.BlockSpec(memory_space=pltpu.VMEM),
         scratch_shapes=[
+            pltpu.VMEM((2, step, depth), f32),
+            pltpu.VMEM((owned, depth), bf16),
+            pltpu.VMEM((owned, depth), bf16),
+            pltpu.VMEM((3, count, depth), f32),
+            pltpu.VMEM((8 * LANES, depth), bf16),
+            pltpu.VMEM((2, h, 2, 2, h, 4 * LANES), f32),
             pltpu.VMEM((4, 2, h, 2, h, LANES), f32),
             pltpu.VMEM((3, 2 * quad, LANES), f32),
             pltpu.VMEM((8 * quad, LANES), f32),
@@ -304,29 +476,21 @@
             pltpu.VMEM((4, quad, LANES), f32),
             pltpu.VMEM((2, 2, h * h, LANES), f32),
             pltpu.VMEM((2, h * h, LANES), f32),
+            dma((2,)), dma((3, 2)), dma((3, 2)),
             dma((4, 2)), dma((4, 2)), dma((3,)), dma((3,)),
             dma((4,)), dma((4,)), dma((4,)), dma((4,)), dma, dma,
         ],
         compiler_params=pltpu.CompilerParams(
-            collective_id=0, has_side_effects=True, vmem_limit_bytes=48 * 1024 * 1024
+            collective_id=0, has_side_effects=True, vmem_limit_bytes=60 * 1024 * 1024
         ),
-        name="reduce_antisymmetrized",
-    )(ct)
+        name="ladder",
+    )(amplitudes, integrals)
 
 
 def block_body(amplitudes, integrals, eps_occ, eps_vir, pair_list):
     tile_width = eps_vir.shape[0] // 2
     count = amplitudes.shape[0]
-    gathered = lax.all_gather(amplitudes, "pair", axis=0, tiled=False)
-    gathered = jnp.pad(gathered, ((0, 0), (0, LANES - count), (0, 0)))
-    ct = lax.dot_general(
-        integrals,
-        gathered.reshape(-1, gathered.shape[2]),
-        (((1,), (1,)), ((), ())),
-        precision=lax.Precision.HIGH,
-        preferred_element_type=jnp.float32,
-    )
-    ladder = reduced(ct, tile_width).T[:count]
+    ladder = ladder_of(amplitudes, integrals, tile_width).T[:count]
     return (ladder, updated(ladder, eps_occ, eps_vir, pair_list))
 
 

time: 161 us -> 95.4 us (0.59)
  the two profiles are of different devices: /device:TPU:17 before, /device:TPU:7 now
where the time goes in v2:
time: 95.4 us; the launch traced here: 95.1 us
  Pallas kernels  89.4 us (94%)
  local copies, waits for them, and re-layouts  2.81 us (3%)
  other arithmetic  2.22 us (2%)
    pallas_call x1, Pallas kernels, ladder_of(): pl.pallas_call(functools.partial(ladder_kernel, h), out_shape=jax.ShapeDt...  89.4 us
    unnamed x2, local copies, waits for them, and re-layouts  1.96 us

profile of v2, /device:TPU:7, one launch (start us, length us, event | category | flops | bytes accessed | tf_op | source)
XLA Modules:
  0.0 95.1 jit_solution(11652515242733672237)
XLA Ops:
  0.6 0.9 select_reduce_fusion
  1.5 0.7 add.22
  2.3 0.1 broadcast_add_fusion
  2.4 0.1 add.26
  2.5 89.4 %ladder.1 = f32[1024,128]{1,0:T(8,128)} custom-call(f32[120,1536]{1,0:T(8,128)} %amp_ref.1, f32[2048,1536]{1,0:T(8,128)} %int_ref.1), custom_call_target="tpu_custom_call" | custom-call | tf_op jit(solution)/shard_map/ladder/pallas_call | solution.py:457
  91.9 1.2 %subtract_divide_fusion = (f32[120,1024]{0,1:T(8,128)S(1)}, f32[120,1024]{0,1:T(8,128)S(1)}) fusion(f32[1024]{0:T(1024)S(1)} %dynamic_slice.3, f32[120]{0:T(128)S(1)} %select_reduce_fusion, f32[128,1024]{0,1:T(8,128)} %bitcast.1), kind=kLoop, calls=%fused_computation | loop fusion | flops 245760 | bytes 1479136 | tf_op jit(solution)/shard_map/div | solution.py:41
  93.2 1.0 %copy.11 = f32[120,1024]{1,0:T(8,128)} copy(f32[120,1024]{0,1:T(8,128)S(1)} %get-tuple-element.6) | data formatting | bytes 983040
  94.2 1.0 %copy.10 = f32[120,1024]{1,0:T(8,128)} copy(f32[120,1024]{0,1:T(8,128)S(1)} %get-tuple-element.7) | data formatting | bytes 983040
  (2 shorter events, 0.0 us)

commit v3 on v2

--- a/solution.py
+++ b/solution.py
@@ -68,7 +68,7 @@
 
 def ladder_kernel(
     h, amp_ref, int_ref, out_ref, stage, int_high, int_low, blocks, weights, ct_ref,
-    got, summed, rows, diff, below, above, upward, downward, kept, other,
+    got, summed, rows, diff, below, above, upward, downward, kept, other, placed,
     stage_sem, amp_send, amp_recv,
     core_send, core_recv, pair_send, pair_recv, up_send, up_recv, down_send, down_recv,
     last_send, last_recv,
@@ -81,7 +81,6 @@
     x = r % 2
     y = r // 2
     peers = (y * 2 + (1 - x), (1 - y) * 2 + x, (1 - y) * 2 + (1 - x))
-    quad = 2 * h * h
     count, depth = amp_ref.shape
     cut = count // 16 * 8
     parts = (pl.ds(0, cut), pl.ds(cut, count - cut))
@@ -203,15 +202,19 @@
             device_id_type=MESH,
         )
 
-    def pair_copy(n):
+    def pair_copy(n, piece):
+        bh = jnp.where(piece == 0, 1 - x, x) if n == 1 else piece
         return pltpu.make_async_remote_copy(
-            src_ref=summed.at[n],
-            dst_ref=rows.at[pl.ds(pl.multiple_of(r * 2 * quad, 8), 2 * quad)],
-            send_sem=pair_send.at[n],
-            recv_sem=pair_recv.at[n],
+            src_ref=summed.at[n, :, bh],
+            dst_ref=rows.at[r, :, bh],
+            send_sem=pair_send.at[n, piece],
+            recv_sem=pair_recv.at[n, piece],
             device_id={"pair": order[n]},
             device_id_type=MESH,
         )
+
+    def pair_arrived(n, piece):
+        pair_copy(n, piece).wait_recv()
 
     def core_start(n):
         for i in range(2):
@@ -222,16 +225,14 @@
         for i in range(2):
             core_copy(n, i).wait_recv()
 
-            @pl.loop(0, h)
+            @pl.loop(0, h, unroll=4)
             def _(a):
                 for bh in range(2):
                     total = ct_ref[i, a, bh, (c + i) % 2, :, lanes] + got[n, i, a, bh]
-                    start = ((i * h + a) * 2 + bh) * h
                     if n < 3:
-                        summed[n, pl.ds(pl.multiple_of(start, 8), h), :] = total
+                        summed[n, i * h + a, bh] = total
                     else:
-                        at = pl.multiple_of(r * 2 * quad + start, 8)
-                        rows[pl.ds(at, h), :] = total
+                        rows[r, i * h + a, bh] = total
 
     core_start(3)
     for d in range(2):
@@ -251,9 +252,12 @@
     core_start(1)
     core_start(2)
     core_add(3)
-    for n in (1, 2):
-        core_add(n)
-        pair_copy(n).start()
+    core_add(1)
+    pair_copy(1, 0).start()
+    core_add(2)
+    pair_copy(2, 0).start()
+    pair_copy(2, 1).start()
+    pair_copy(1, 1).start()
     for d in range(2):
         pass_on(d).wait_recv()
     weigh(blocks.at[2], 2, 3)
@@ -265,22 +269,19 @@
 
     core_start(0)
     core_add(0)
-    pair_copy(0).start()
-
-    def antisym(q):
+    pair_copy(0, 0).start()
+    pair_copy(0, 1).start()
+
+    def antisym(q, i):
         ah = q // 2
         bh = q % 2
-        for i in range(2):
-            mirror = (c + i) % 2
-
-            @pl.loop(0, h)
-            def _(a):
-                direct = (((ah * 2 + i) * h + a) * 2 + bh) * h
-                swapped = ((((2 + bh) * 2 + mirror) * h) * 2 + ah) * h + a
-                plain = rows[pl.ds(pl.multiple_of(direct, 8), h), :]
-                turned = rows[pl.ds(swapped, h, stride=2 * h), :]
-                at = pl.multiple_of((i * h + a) * h, 8)
-                diff[q, pl.ds(at, h), :] = plain - turned
+        mirror = (c + i) % 2
+
+        @pl.loop(0, h, unroll=4)
+        def _(a):
+            plain = rows[ah, i * h + a, bh]
+            turned = rows[2 + bh, pl.ds(mirror * h, h), ah, a, :]
+            diff[q * 2 + i, pl.ds(pl.multiple_of(a * h, 8), h), :] = plain - turned
 
     def up_copy(q):
         return pltpu.make_async_remote_copy(
@@ -297,16 +298,16 @@
         )
 
     def sends_up(q):
-        return jnp.logical_or(z < 2, jnp.logical_and(z == 2, q % 2 == 1))
+        return jnp.logical_or(z < 2, jnp.logical_and(z == 2, q // 2 % 2 == 1))
 
     def sends_down(q):
-        return jnp.logical_or(z > 1, jnp.logical_and(z == 1, q // 2 == 0))
+        return jnp.logical_or(z > 1, jnp.logical_and(z == 1, q // 4 == 0))
 
     def hears_below(q):
-        return jnp.logical_or(inner, jnp.logical_and(z == 3, q % 2 == 1))
+        return jnp.logical_or(inner, jnp.logical_and(z == 3, q // 2 % 2 == 1))
 
     def hears_above(q):
-        return jnp.logical_or(inner, jnp.logical_and(z == 0, q // 2 == 0))
+        return jnp.logical_or(inner, jnp.logical_and(z == 0, q // 4 == 0))
 
     def go_up(q):
         @pl.when(hears_below(q))
@@ -362,42 +363,35 @@
 
     early = [jnp.where(y == 0, t * 2 + x, x * 2 + t) for t in range(2)]
     late = [jnp.where(y == 0, t * 2 + 1 - x, (1 - x) * 2 + t) for t in range(2)]
-    pair_copy(1).wait_recv()
-    pair_copy(2).wait_recv()
-    antisym(early[0])
-    near(early[0])
-    antisym(early[1])
-    near(early[1])
-
-    @pl.when(inner)
-    def _():
-        far(early[0])
-
-    pair_copy(0).wait_recv()
-    antisym(late[0])
-    near(late[0])
-
-    @pl.when(inner)
-    def _():
-        far(early[1])
-
-    antisym(late[1])
-    near(late[1])
+    quads = early + late
+    chunks = [q * 2 + i for q in quads for i in range(2)]
+    needs = (((1, 0), (2, 0)), ((2, 1),), ((1, 1), (0, 0)), ((0, 1),))
+    lag = 2
+    for s in range(8):
+        if s % 2 == 0:
+            for n, piece in needs[s // 2]:
+                pair_arrived(n, piece)
+        antisym(quads[s // 2], s % 2)
+        near(chunks[s])
+        if s >= lag:
+
+            @pl.when(inner)
+            def _():
+                far(chunks[s - lag])
 
     @pl.when(jnp.logical_not(inner))
     def _():
-        far(early[0])
-        far(early[1])
-
-    far(late[0])
-    far(late[1])
+        for s in range(8 - lag):
+            far(chunks[s])
+
+    for s in range(8 - lag, 8):
+        far(chunks[s])
 
     def total_of(t, i):
-        q = jnp.where(z < 2, z * 2 + t, t * 2 + z - 2)
-        at = pl.ds(pl.multiple_of(i * h * h, 8), h * h)
-        low = jnp.where(z > 0, below[q, at, :], jnp.float32(0.0))
-        high = jnp.where(z < 3, above[q, at, :], jnp.float32(0.0))
-        return diff[q, at, :] + low + high
+        q = jnp.where(z < 2, z * 2 + t, t * 2 + z - 2) * 2 + i
+        low = jnp.where(z > 0, below[q], jnp.float32(0.0))
+        high = jnp.where(z < 3, above[q], jnp.float32(0.0))
+        return diff[q] + low + high
 
     mine = jnp.where(z < 2, c, 0)
     for t in range(2):
@@ -413,16 +407,20 @@
     def put(s):
         for t in range(2):
 
-            @pl.loop(0, h)
+            @pl.loop(0, h, unroll=4)
             def _(a):
                 at = pl.multiple_of((a * 4 + 2 * t + s) * h, 8)
                 plain = kept[s, t, pl.ds(pl.multiple_of(a * h, 8), h), :]
                 turned = kept[s, t, pl.ds(a, h, stride=h), :]
-                out_ref[pl.ds(at, h), :] = jnp.where(z < 2, plain, -turned)
+                placed[pl.ds(at, h), :] = jnp.where(z < 2, plain, -turned)
 
     put(0)
     last.wait_recv()
     put(1)
+
+    for n in range(out_ref.shape[1] // LANES):
+        at = pl.ds(n * LANES, LANES)
+        out_ref[:, at] = placed[at, :].T[:count]
 
     last.wait_send()
     for d in range(2):
@@ -433,8 +431,9 @@
         for i in range(2):
             core_copy(n, i).wait_send()
     for n in range(3):
-        pair_copy(n).wait_send()
-    for q in range(4):
+        for piece in range(2):
+            pair_copy(n, piece).wait_send()
+    for q in range(8):
 
         @pl.when(sends_up(q))
         def _():
@@ -447,7 +446,6 @@
 
 def ladder_of(amplitudes, integrals, tile_width):
     h = tile_width // 4
-    quad = 2 * h * h
     count, depth = amplitudes.shape
     owned = integrals.shape[0]
     step = owned // 8
@@ -456,7 +454,7 @@
     dma = pltpu.SemaphoreType.DMA
     return pl.pallas_call(
         functools.partial(ladder_kernel, h),
-        out_shape=jax.ShapeDtypeStruct((tile_width * h, LANES), f32),
+        out_shape=jax.ShapeDtypeStruct((count, tile_width * h), f32),
         in_specs=[pl.BlockSpec(memory_space=pltpu.VMEM), pl.BlockSpec(memory_space=pl.ANY)],
         out_specs=pl.BlockSpec(memory_space=pltpu.VMEM),
         scratch_shapes=[
@@ -467,18 +465,19 @@
             pltpu.VMEM((8 * LANES, depth), bf16),
             pltpu.VMEM((2, h, 2, 2, h, 4 * LANES), f32),
             pltpu.VMEM((4, 2, h, 2, h, LANES), f32),
-            pltpu.VMEM((3, 2 * quad, LANES), f32),
-            pltpu.VMEM((8 * quad, LANES), f32),
-            pltpu.VMEM((4, quad, LANES), f32),
-            pltpu.VMEM((4, quad, LANES), f32),
-            pltpu.VMEM((4, quad, LANES), f32),
-            pltpu.VMEM((4, quad, LANES), f32),
-            pltpu.VMEM((4, quad, LANES), f32),
+            pltpu.VMEM((3, 2 * h, 2, h, LANES), f32),
+            pltpu.VMEM((4, 2 * h, 2, h, LANES), f32),
+            pltpu.VMEM((8, h * h, LANES), f32),
+            pltpu.VMEM((8, h * h, LANES), f32),
+            pltpu.VMEM((8, h * h, LANES), f32),
+            pltpu.VMEM((8, h * h, LANES), f32),
+            pltpu.VMEM((8, h * h, LANES), f32),
             pltpu.VMEM((2, 2, h * h, LANES), f32),
             pltpu.VMEM((2, h * h, LANES), f32),
+            pltpu.VMEM((tile_width * h, LANES), f32),
             dma((2,)), dma((3, 2)), dma((3, 2)),
-            dma((4, 2)), dma((4, 2)), dma((3,)), dma((3,)),
-            dma((4,)), dma((4,)), dma((4,)), dma((4,)), dma, dma,
+            dma((4, 2)), dma((4, 2)), dma((3, 2)), dma((3, 2)),
+            dma((8,)), dma((8,)), dma((8,)), dma((8,)), dma, dma,
         ],
         compiler_params=pltpu.CompilerParams(
             collective_id=0, has_side_effects=True, vmem_limit_bytes=60 * 1024 * 1024
@@ -489,8 +488,7 @@
 
 def block_body(amplitudes, integrals, eps_occ, eps_vir, pair_list):
     tile_width = eps_vir.shape[0] // 2
-    count = amplitudes.shape[0]
-    ladder = ladder_of(amplitudes, integrals, tile_width).T[:count]
+    ladder = ladder_of(amplitudes, integrals, tile_width)
     return (ladder, updated(ladder, eps_occ, eps_vir, pair_list))
 
 

time: 95.4 us -> 81.3 us (0.85)
  the two profiles are of different devices: /device:TPU:7 before, /device:TPU:24 now
where the time goes in v3:
time: 81.3 us; the launch traced here: 81.1 us
  Pallas kernels  76.1 us (94%)
  other arithmetic  2.22 us (3%)
  local copies, waits for them, and re-layouts  2.05 us (3%)
    pallas_call x1, Pallas kernels, ladder_of(): pl.pallas_call(functools.partial(ladder_kernel, h), out_shape=jax.ShapeDt...  76.1 us
    div x1, other arithmetic, updated(): return ladder / (pair_energy[:, None] - local_energy[None, :])  1.96 us
    unnamed x7, local copies, waits for them, and re-layouts  1.86 us

profile of v3, /device:TPU:24, one launch (start us, length us, event | category | flops | bytes accessed | tf_op | source)
XLA Modules:
  0.0 81.1 jit_solution(847294055598962992)
XLA Ops:
  0.6 0.0 copy-start.2
  0.6 0.0 copy-start.1
  0.7 0.0 copy-start
  0.7 76.1 %ladder.1 = f32[120,1024]{1,0:T(8,128)} custom-call(f32[120,1536]{1,0:T(8,128)} %amp_ref.1, f32[2048,1536]{1,0:T(8,128)} %int_ref.1), custom_call_target="tpu_custom_call" | custom-call | tf_op jit(solution)/shard_map/ladder/pallas_call | solution.py:455
  76.8 0.0 copy-done.2
  76.8 0.1 add.22
  76.9 0.1 broadcast_add_fusion
  77.0 0.1 add.26
  77.1 0.0 copy-done.1
  77.1 0.0 copy-done
  77.1 0.2 select_reduce_fusion
  77.2 2.0 %subtract_divide_fusion = f32[120,1024]{1,0:T(8,128)} fusion(f32[120,1024]{1,0:T(8,128)} %ladder.1, f32[1024]{0:T(1024)S(1)} %dynamic_slice.3, f32[120]{0:T(128)S(1)} %select_reduce_fusion), kind=kLoop, calls=%fused_computation | loop fusion | flops 245760 | bytes 987616 | tf_op jit(solution)/shard_map/div | solution.py:41
  79.2 1.9 %copy.9 = f32[120,1024]{1,0:T(8,128)} copy(f32[120,1024]{1,0:T(8,128)} %ladder.1) | data formatting | bytes 983040
  (2 shorter events, 0.0 us)
Async XLA Ops:
  0.6 76.1 %copy-start.2 = (f32[128]{0:T(128)S(1)}, f32[128]{0:T(128)}, u32[]{:S(2)}) copy-start(f32[128]{0:T(128)} %param.8) | copy-start | bytes 1540
  0.6 76.4 %copy-start.1 = (f32[120]{0:T(128)S(1)}, f32[120]{0:T(128)}, u32[]{:S(2)}) copy-start(f32[120]{0:T(128)} %param.7) | copy-start | bytes 1444
  0.7 76.4 %copy-start = (s32[120,2]{0,1:T(2,128)S(1)}, s32[120,2]{0,1:T(2,128)}, u32[]{:S(2)}) copy-start(s32[120,2]{0,1:T(2,128)} %param.9) | copy-start | bytes 2884

commit v4 on v3

--- a/solution.py
+++ b/solution.py
@@ -220,6 +220,8 @@
         for i in range(2):
             core_copy(n, i).start()
 
+    half = steps // 4
+
     def core_add(n):
         lanes = pl.ds(n * LANES, LANES)
         for i in range(2):
@@ -240,24 +242,27 @@
         weigh(blocks.at[d], 4 + d, 6 + d)
     big = 2 * step
 
-    @pl.loop(0, steps // 2)
-    def _(t):
-        at = pl.ds(pl.multiple_of(t * big, 16), big)
-        near_high = weights[pl.ds(4 * LANES, 2 * LANES), :]
-        near_low = weights[pl.ds(6 * LANES, 2 * LANES), :]
-        value = times(int_high[at, :], near_high) + times(int_high[at, :], near_low)
-        value = value + times(int_low[at, :], near_high)
-        keep(t, big, pl.ds(LANES, 2 * LANES), value)
-
-    core_start(1)
-    core_start(2)
-    core_add(3)
+    for i in range(2):
+
+        @pl.loop(i * half, (i + 1) * half)
+        def _(t):
+            at = pl.ds(pl.multiple_of(t * big, 16), big)
+            near_high = weights[pl.ds(4 * LANES, 2 * LANES), :]
+            near_low = weights[pl.ds(6 * LANES, 2 * LANES), :]
+            value = times(int_high[at, :], near_high) + times(int_high[at, :], near_low)
+            value = value + times(int_low[at, :], near_high)
+            keep(t, big, pl.ds(LANES, 2 * LANES), value)
+
+        core_copy(1, i).start()
+        core_copy(2, i).start()
+
     core_add(1)
     pair_copy(1, 0).start()
     core_add(2)
     pair_copy(2, 0).start()
     pair_copy(2, 1).start()
     pair_copy(1, 1).start()
+    core_add(3)
     for d in range(2):
         pass_on(d).wait_recv()
     weigh(blocks.at[2], 2, 3)
@@ -272,16 +277,17 @@
     pair_copy(0, 0).start()
     pair_copy(0, 1).start()
 
-    def antisym(q, i):
+    def antisym(q, i, u):
         ah = q // 2
         bh = q % 2
         mirror = (c + i) % 2
 
-        @pl.loop(0, h, unroll=4)
-        def _(a):
+        @pl.loop(0, h // 2, unroll=4)
+        def _(n):
+            a = u * (h // 2) + n
             plain = rows[ah, i * h + a, bh]
             turned = rows[2 + bh, pl.ds(mirror * h, h), ah, a, :]
-            diff[q * 2 + i, pl.ds(pl.multiple_of(a * h, 8), h), :] = plain - turned
+            diff[q * 4 + i * 2 + u, pl.ds(pl.multiple_of(n * h, 8), h), :] = plain - turned
 
     def up_copy(q):
         return pltpu.make_async_remote_copy(
@@ -298,16 +304,16 @@
         )
 
     def sends_up(q):
-        return jnp.logical_or(z < 2, jnp.logical_and(z == 2, q // 2 % 2 == 1))
+        return jnp.logical_or(z < 2, jnp.logical_and(z == 2, q // 4 % 2 == 1))
 
     def sends_down(q):
-        return jnp.logical_or(z > 1, jnp.logical_and(z == 1, q // 4 == 0))
+        return jnp.logical_or(z > 1, jnp.logical_and(z == 1, q // 8 == 0))
 
     def hears_below(q):
-        return jnp.logical_or(inner, jnp.logical_and(z == 3, q // 2 % 2 == 1))
+        return jnp.logical_or(inner, jnp.logical_and(z == 3, q // 4 % 2 == 1))
 
     def hears_above(q):
-        return jnp.logical_or(inner, jnp.logical_and(z == 0, q // 4 == 0))
+        return jnp.logical_or(inner, jnp.logical_and(z == 0, q // 8 == 0))
 
     def go_up(q):
         @pl.when(hears_below(q))
@@ -364,14 +370,14 @@
     early = [jnp.where(y == 0, t * 2 + x, x * 2 + t) for t in range(2)]
     late = [jnp.where(y == 0, t * 2 + 1 - x, (1 - x) * 2 + t) for t in range(2)]
     quads = early + late
-    chunks = [q * 2 + i for q in quads for i in range(2)]
+    chunks = [q * 4 + n for q in quads for n in range(4)]
     needs = (((1, 0), (2, 0)), ((2, 1),), ((1, 1), (0, 0)), ((0, 1),))
-    lag = 2
-    for s in range(8):
-        if s % 2 == 0:
-            for n, piece in needs[s // 2]:
+    lag = 3
+    for s in range(16):
+        if s % 4 == 0:
+            for n, piece in needs[s // 4]:
                 pair_arrived(n, piece)
-        antisym(quads[s // 2], s % 2)
+        antisym(quads[s // 4], s // 2 % 2, s % 2)
         near(chunks[s])
         if s >= lag:
 
@@ -381,17 +387,17 @@
 
     @pl.when(jnp.logical_not(inner))
     def _():
-        for s in range(8 - lag):
+        for s in range(16 - lag):
             far(chunks[s])
 
-    for s in range(8 - lag, 8):
+    for s in range(16 - lag, 16):
         far(chunks[s])
 
     def total_of(t, i):
-        q = jnp.where(z < 2, z * 2 + t, t * 2 + z - 2) * 2 + i
+        q = pl.ds(jnp.where(z < 2, z * 2 + t, t * 2 + z - 2) * 4 + i * 2, 2)
         low = jnp.where(z > 0, below[q], jnp.float32(0.0))
         high = jnp.where(z < 3, above[q], jnp.float32(0.0))
-        return diff[q] + low + high
+        return (diff[q] + low + high).reshape(h * h, LANES)
 
     mine = jnp.where(z < 2, c, 0)
     for t in range(2):
@@ -412,7 +418,7 @@
                 at = pl.multiple_of((a * 4 + 2 * t + s) * h, 8)
                 plain = kept[s, t, pl.ds(pl.multiple_of(a * h, 8), h), :]
                 turned = kept[s, t, pl.ds(a, h, stride=h), :]
-                placed[pl.ds(at, h), :] = jnp.where(z < 2, plain, -turned)
+                placed[pl.ds(at, h), :] = jnp.where(z < 2, plain, turned)
 
     put(0)
     last.wait_recv()
@@ -433,7 +439,7 @@
     for n in range(3):
         for piece in range(2):
             pair_copy(n, piece).wait_send()
-    for q in range(8):
+    for q in range(16):
 
         @pl.when(sends_up(q))
         def _():
@@ -467,17 +473,17 @@
             pltpu.VMEM((4, 2, h, 2, h, LANES), f32),
             pltpu.VMEM((3, 2 * h, 2, h, LANES), f32),
             pltpu.VMEM((4, 2 * h, 2, h, LANES), f32),
-            pltpu.VMEM((8, h * h, LANES), f32),
-            pltpu.VMEM((8, h * h, LANES), f32),
-            pltpu.VMEM((8, h * h, LANES), f32),
-            pltpu.VMEM((8, h * h, LANES), f32),
-            pltpu.VMEM((8, h * h, LANES), f32),
+            pltpu.VMEM((16, h * h // 2, LANES), f32),
+            pltpu.VMEM((16, h * h // 2, LANES), f32),
+            pltpu.VMEM((16, h * h // 2, LANES), f32),
+            pltpu.VMEM((16, h * h // 2, LANES), f32),
+            pltpu.VMEM((16, h * h // 2, LANES), f32),
             pltpu.VMEM((2, 2, h * h, LANES), f32),
             pltpu.VMEM((2, h * h, LANES), f32),
             pltpu.VMEM((tile_width * h, LANES), f32),
             dma((2,)), dma((3, 2)), dma((3, 2)),
             dma((4, 2)), dma((4, 2)), dma((3, 2)), dma((3, 2)),
-            dma((8,)), dma((8,)), dma((8,)), dma((8,)), dma, dma,
+            dma((16,)), dma((16,)), dma((16,)), dma((16,)), dma, dma,
         ],
         compiler_params=pltpu.CompilerParams(
             collective_id=0, has_side_effects=True, vmem_limit_bytes=60 * 1024 * 1024
@@ -488,7 +494,9 @@
 
 def block_body(amplitudes, integrals, eps_occ, eps_vir, pair_list):
     tile_width = eps_vir.shape[0] // 2
-    ladder = ladder_of(amplitudes, integrals, tile_width)
+    first = lax.axis_index("virt") < lax.axis_size("virt") // 2
+    sign = jnp.where(first, jnp.float32(1.0), jnp.float32(-1.0))
+    ladder = sign * ladder_of(amplitudes, integrals, tile_width)
     return (ladder, updated(ladder, eps_occ, eps_vir, pair_list))
 
 

time: 81.3 us -> 79.3 us (0.975)
  Pallas kernels: 76.1 us -> 74.5 us
  local copies, waits for them, and re-layouts: 2.05 us -> 0.85 us
    unnamed x7 -> x0, local copies, waits for them, and re-layouts: 1.86 us -> none
    pallas_call x1, Pallas kernels: 76.1 us -> 74.5 us  [ladder_of(): pl.pallas_call(functools.partial(ladder_kernel, h), out_shape=jax.ShapeDt...]
where the time goes in v4:
time: 79.3 us; the launch traced here: 79 us
  Pallas kernels  74.5 us (94%)
  other arithmetic  3.01 us (4%)
  local copies, waits for them, and re-layouts  0.85 us (1%)
    pallas_call x1, Pallas kernels, ladder_of(): pl.pallas_call(functools.partial(ladder_kernel, h), out_shape=jax.ShapeDt...  74.5 us
    div x1, other arithmetic, updated(): return ladder / (pair_energy[:, None] - local_energy[None, :])  2.03 us

profile of v4, /device:TPU:24, one launch (start us, length us, event | category | flops | bytes accessed | tf_op | source)
XLA Modules:
  0.0 79.0 jit_solution(17536102911710693920)
XLA Ops:
  0.6 0.9 %select_reduce_fusion = f32[120]{0:T(128)S(1)} fusion(f32[120]{0:T(128)} %param.7, s32[120,2]{0,1:T(2,128)} %param.9), kind=kLoop, calls=%fused_computation.2 | loop fusion | flops 86280 | bytes 1920 | tf_op jit(solution)/shard_map/reduce_sum | solution.py:23
  1.5 0.7 add.22
  2.3 0.1 broadcast_add_fusion
  2.4 0.1 add.26
  2.5 74.5 %ladder.1 = f32[120,1024]{1,0:T(8,128)} custom-call(f32[120,1536]{1,0:T(8,128)} %amp_ref.1, f32[2048,1536]{1,0:T(8,128)} %int_ref.1), custom_call_target="tpu_custom_call" | custom-call | tf_op jit(solution)/shard_map/ladder/pallas_call | solution.py:461
  77.0 2.0 %subtract_divide_fusion = (f32[120,1024]{1,0:T(8,128)}, f32[120,1024]{1,0:T(8,128)}) fusion(f32[1024]{0:T(1024)S(1)} %dynamic_slice.3, f32[120]{0:T(128)S(1)} %select_reduce_fusion, f32[120,1024]{1,0:T(8,128)} %ladder.1, f32[]{:T(128)S(6)} %select_n.11), kind=kLoop, calls=%fused_computation | loop fusion | flops 368640 | bytes 1479140 | tf_op jit(solution)/shard_map/div | solution.py:41
  (2 shorter events, 0.0 us)

commit v5 on v4

--- a/solution.py
+++ b/solution.py
@@ -496,7 +496,11 @@
     tile_width = eps_vir.shape[0] // 2
     first = lax.axis_index("virt") < lax.axis_size("virt") // 2
     sign = jnp.where(first, jnp.float32(1.0), jnp.float32(-1.0))
-    ladder = sign * ladder_of(amplitudes, integrals, tile_width)
+    raw = ladder_of(amplitudes, integrals, tile_width)
+    raw, eps_occ, eps_vir, pair_list = lax.optimization_barrier(
+        (raw, eps_occ, eps_vir, pair_list)
+    )
+    ladder = sign * raw
     return (ladder, updated(ladder, eps_occ, eps_vir, pair_list))
 
 

time: 79.3 us -> 78 us (0.984)
  no operation moved by 1% of the time
where the time goes in v5:
time: 78 us; the launch traced here: 77.7 us
  Pallas kernels  74.6 us (96%)
  other arithmetic  2.29 us (3%)
    pallas_call x1, Pallas kernels, ladder_of(): pl.pallas_call(functools.partial(ladder_kernel, h), out_shape=jax.ShapeDt...  74.6 us
    div x1, other arithmetic, updated(): return ladder / (pair_energy[:, None] - local_energy[None, :])  2.03 us

profile of v5, /device:TPU:24, one launch (start us, length us, event | category | flops | bytes accessed | tf_op | source)
XLA Modules:
  0.0 77.7 jit_solution(15468828725705680275)
XLA Ops:
  0.6 0.0 copy-start
  0.6 0.0 copy-start.2
  0.7 0.0 copy-start.1
  0.7 74.6 %ladder.1 = f32[120,1024]{1,0:T(8,128)} custom-call(f32[120,1536]{1,0:T(8,128)} %amp_ref.1, f32[2048,1536]{1,0:T(8,128)} %int_ref.1), custom_call_target="tpu_custom_call" | custom-call | tf_op jit(solution)/shard_map/ladder/pallas_call | solution.py:461
  75.2 0.0 copy-done
  75.2 0.0 copy-done.1
  75.3 0.2 select_reduce_fusion
  75.4 0.0 copy-done.2
  75.4 0.1 add.22
  75.6 0.1 broadcast_add_fusion
  75.6 0.1 add.26
  75.7 2.0 %subtract_divide_fusion = (f32[120,1024]{1,0:T(8,128)}, f32[120,1024]{1,0:T(8,128)}) fusion(f32[1024]{0:T(1024)S(1)} %dynamic_slice.3, f32[120]{0:T(128)S(1)} %select_reduce_fusion, f32[120,1024]{1,0:T(8,128)} %ladder.1, f32[]{:T(128)S(6)} %select_n.11), kind=kLoop, calls=%fused_computation | loop fusion | flops 368640 | bytes 1479140 | tf_op jit(solution)/shard_map/div | solution.py:41
  (2 shorter events, 0.0 us)
Async XLA Ops:
  0.6 74.6 %copy-start = (s32[120,2]{0,1:T(2,128)S(1)}, s32[120,2]{0,1:T(2,128)}, u32[]{:S(2)}) copy-start(s32[120,2]{0,1:T(2,128)} %param.9) | copy-start | bytes 2884
  0.6 74.8 %copy-start.2 = (f32[128]{0:T(128)S(1)}, f32[128]{0:T(128)}, u32[]{:S(2)}) copy-start(f32[128]{0:T(128)} %param.8) | copy-start | bytes 1540
  0.7 74.6 %copy-start.1 = (f32[120]{0:T(128)S(1)}, f32[120]{0:T(128)}, u32[]{:S(2)}) copy-start(f32[120]{0:T(128)} %param.7) | copy-start | bytes 1444
